TPU v7x, 128 devices: a whole 4x4x4 slice. The times are simulated.
128 devices in a mesh: grp: 64 (over z, y, x), sub: 2 (over core).
Axes of the slice: x: 4, y: 4, z: 4, core: 2. Of those that a mesh axis runs over, the one named last changes fastest.
Arguments:
- potentials: bfloat16 [4096, 200, 200], P(('grp', 'sub')), may hold values from -6 to 6
- dimers: int32 [16384, 2], P(('grp', 'sub')), may hold values from 0 to 4095, as said below
- coupling: float32 [16384], P(('grp', 'sub')), may hold values from 0.3 to 1.5
- transform: bfloat16 [400, 400], replicated, may hold values from -0.3125 to 0.3125
Outputs:
- energies: float32 [16384, 400], P(('grp', 'sub'))
- checksum: float32 [1], replicated
Inputs may be any that keep to these rules, and one draw needn't show every extreme that they name: `dimers`: each row names two different fragments. Rows d with d // 128 = o belong to owner o, and their second fragment f has f // 32 = o. Among the 128 first fragments of one owner's rows, at most 2 fall into the fragments of any one device (fragments f with f // 32 equal), and exactly 2 into some device's fragments.
All inputs are finite; a program needn't handle non-finite values.
Results may differ from a plain program's by a relative error of at most 0.0023.
Values may be sent and summed in bfloat16 or wider, within the bound.
A program may use at most 192 MiB of HBM per device.

v0:
```python
import jax
import jax.numpy as jnp
from jax import lax
from jax.sharding import Mesh
from jax.sharding import PartitionSpec as P

GRP_SUB = ("grp_0", "grp_1", "grp_2", "sub")


def in_blocks(value, dim, peers):
    before, after = (value.shape[:dim], value.shape[dim + 1 :])
    return jnp.moveaxis(value.reshape(*before, peers, -1, *after), dim, 0)


def edges_of(length, count):
    unit = 8 if length >= 8 * count else 1
    return [length // unit * k // count * unit for k in range(1, count)]


def in_order(tiles, dim):
    tiles = jnp.moveaxis(tiles, 0, dim)
    shape = tiles.shape
    return tiles.reshape(*shape[:dim], shape[dim] * shape[dim + 1], *shape[dim + 2 :])


def several_exchanges(value, axis, pieces, split_dim, concat_dim):
    tiles = in_blocks(value, split_dim, lax.axis_size(axis))
    widest = max(range(1, max(2, tiles.ndim - 1)), key=lambda d: tiles.shape[d])
    done = []
    for section in jnp.split(tiles, edges_of(tiles.shape[widest], pieces), axis=widest):
        if section.size:
            done.append(lax.all_to_all(section, axis, split_axis=0, concat_axis=0, tiled=True))
    return in_order(jnp.concatenate(done, axis=widest), concat_dim)


def over_axes(value, axes):
    for axis in axes:
        value = lax.psum(value, axis)
    return value


def block_energies(left, right, scale, transform, basis):
    upper = transform[:basis]
    lower = transform[basis:]
    cross = jnp.einsum("nab,nbc->nac", left, right, preferred_element_type=jnp.float32)
    block = (cross * (scale[:, None, None] / jnp.sqrt(jnp.float32(basis)))).astype(jnp.bfloat16)
    top = jnp.einsum("nab,bk->nak", left, upper, preferred_element_type=jnp.float32)
    top = top + jnp.einsum("nab,bk->nak", block, lower, preferred_element_type=jnp.float32)
    bottom = jnp.einsum("nab,ak->nbk", block, upper, preferred_element_type=jnp.float32)
    bottom = bottom + jnp.einsum("nab,bk->nak", right, lower, preferred_element_type=jnp.float32)
    upper_f = upper.astype(jnp.float32)
    lower_f = lower.astype(jnp.float32)
    return jnp.sum(upper_f[None] * top, axis=1) + jnp.sum(lower_f[None] * bottom, axis=1)


def local(potentials, dimers, coupling, transform):
    frag_dev, basis, _ = potentials.shape
    count = dimers.shape[0]
    owners = lax.axis_size(GRP_SUB)
    cap = max(2, (4 * count + 3 * owners - 1) // (3 * owners))
    wanted = dimers[:, 0]
    source = wanted // frag_dev
    onehot = (source[:, None] == jnp.arange(owners, dtype=jnp.int32)[None, :]).astype(jnp.int32)
    ranking = jnp.sum(jnp.cumsum(onehot, axis=0) * onehot, axis=1) - 1
    slots = source * cap + ranking
    requests = jnp.zeros((owners * cap,), jnp.int32).at[slots].set(wanted % frag_dev)
    asked = lax.all_to_all(
        requests.reshape(owners, cap), GRP_SUB, split_axis=0, concat_axis=0, tiled=True
    )
    served = jnp.take(potentials, asked.reshape(-1), axis=0).reshape(owners, cap, basis, basis)
    arrived = several_exchanges(served, GRP_SUB, 2, 0, 0)
    leading = jnp.take(arrived.reshape(owners * cap, basis, basis), slots, axis=0)
    trailing = jnp.take(potentials, dimers[:, 1] % frag_dev, axis=0)
    width = 8
    leading = leading.reshape(count // width, width, basis, basis)
    trailing = trailing.reshape(count // width, width, basis, basis)
    scales = coupling.reshape(count // width, width)

    def one_block(item):
        left, right, scale = item
        return block_energies(left, right, scale, transform, basis)

    energies = lax.map(one_block, (leading, trailing, scales)).reshape(count, 2 * basis)
    total = count * owners
    position = lax.axis_index(GRP_SUB) * count + jnp.arange(count, dtype=jnp.int32)
    weights = (position.astype(jnp.float32) + 1.0) / total
    partial_value = 2.0 / total * jnp.sum(weights * jnp.mean(energies * energies, axis=1))
    checksum = over_axes(partial_value, GRP_SUB)
    return (energies, checksum.reshape(1))


def solution(mesh):
    split = Mesh(
        mesh.devices.reshape(4, 4, 4, mesh.shape["sub"]), ("grp_0", "grp_1", "grp_2", "sub")
    )
    return jax.shard_map(
        local,
        mesh=split,
        in_specs=(P(GRP_SUB, None, None), P(GRP_SUB, None), P(GRP_SUB), P()),
        out_specs=(P(GRP_SUB, None), P()),
        check_vma=False,
    )
```

profile of v0, /device:TPU:1, one launch (start us, length us, event | category | flops | bytes accessed | tf_op | source)
XLA Modules:
  0.0 635.7 jit_solution(10583920919584439760)
XLA Ops:
  5.2 20.9 %all_to_all.19 = s32[128,1,2]{2,1,0:T(1,128)S(1)} all-to-all(s32[128,1,2]{2,1,0:T(1,128)S(1)} %bitcast.76), channel_id=1, replica_groups=mesh['grp_0'=4,'grp_1'=4,'grp_2'=4,'sub'=2] {'grp_0','grp_1','grp_2','sub'}, dimensions={0} | all-to-all | bytes 2048 | tf_op jit(solution)/shard_map/all_to_all | solution.py:67
  27.8 12.6 %gather_fusion = bf16[256,200,200]{2,1,0:T(8,128)(2,1)} fusion(bf16[32,200,200]{2,1,0:T(8,128)(2,1)S(1)} %copy-done, s32[1024]{0:T(1024)S(1)} %pad_clamp_fusion.2), kind=kCustom, calls=%fused_computation | custom fusion | bytes 40961024 | tf_op jit(solution)/shard_map/jit(_take)/gather | solution.py:70
  40.4 18.3 %broadcast_select_fusion = bf16[128,1,2,200,200]{4,3,2,1,0:T(8,128)(2,1)} fusion(bf16[128,1,2,200,200]{4,3,2,1,0:T(8,128)(2,1)} %bitcast.70, pred[128,2]{1,0:T(8,128)(4,1)S(1)} %compare_and_fusion), kind=kLoop, calls=%fused_computation.35 | loop fusion | flops 10240000 | bytes 40960256 | tf_op jit(solution)/shard_map/jit(_take)/select_n | solution.py:70
  58.7 11.0 %split.8 = bf16[128,1,2,96,200]{4,3,2,1,0:T(8,128)(2,1)} slice(bf16[128,1,2,200,200]{4,3,2,1,0:T(8,128)(2,1)} %broadcast_select_fusion), slice={[0:128], [0:1], [0:2], [0:96], [0:200]} | slice | bytes 19660800 | tf_op jit(solution)/shard_map/split | solution.py:30
  69.6 5.5 all-to-all-start.1
  75.1 12.2 %split.9 = bf16[128,1,2,104,200]{4,3,2,1,0:T(8,128)(2,1)} slice(bf16[128,1,2,200,200]{4,3,2,1,0:T(8,128)(2,1)} %broadcast_select_fusion), slice={[0:128], [0:1], [0:2], [96:200], [0:200]} | slice | bytes 21299200 | tf_op jit(solution)/shard_map/split | solution.py:30
  87.3 18.8 %copy.31 = bf16[128,1,2,104,200]{3,4,2,1,0:T(8,128)(2,1)} copy(bf16[128,1,2,104,200]{4,3,2,1,0:T(8,128)(2,1)} %split.9) | data formatting | bytes 21299200 | tf_op jit(solution)/shard_map/split | solution.py:30
  106.1 121.2 %all-to-all-done.1 = bf16[128,1,2,96,200]{4,3,2,1,0:T(8,128)(2,1)} async-done(((bf16[128,1,2,96,200]{4,3,2,1,0:T(8,128)(2,1)}), bf16[128,1,2,96,200]{4,3,2,1,0:T(8,128)(2,1)}, u32[]{:S(2)}, u32[]{:S(2)}) %all-to-all-start.1) | async-done | bytes 9830432 | tf_op jit(solution)/shard_map/all_to_all | solution.py:32
  227.3 24.5 %all-to-all-start.2 = ((bf16[128,1,2,104,200]{3,4,2,1,0:T(8,128)(2,1)}), bf16[128,1,2,104,200]{3,4,2,1,0:T(8,128)(2,1)}, u32[]{:S(2)}, u32[]{:S(2)}) async-start(bf16[128,1,2,104,200]{3,4,2,1,0:T(8,128)(2,1)} %copy.31), calls=%async_computation.2 | async-start | bytes 26214400 | tf_op jit(solution)/shard_map/all_to_all | solution.py:32
  252.6 8.7 %gather_fusion.2 = bf16[128,200,200]{2,1,0:T(8,128)(2,1)} fusion(bf16[32,200,200]{2,1,0:T(8,128)(2,1)S(1)} %copy-done, s32[1024]{0:T(1024)S(1)} %pad_clamp_fusion), kind=kCustom, calls=%fused_computation.2 | custom fusion | bytes 20480512 | tf_op jit(solution)/shard_map/jit(_take)/gather | solution.py:73
  262.1 10.1 %broadcast_select_fusion.1 = bf16[16,8,200,200]{3,2,1,0:T(8,128)(2,1)} fusion(bf16[16,8,200,200]{3,2,1,0:T(8,128)(2,1)} %bitcast.73, pred[16,8]{1,0:T(8,128)(4,1)S(1)} %broadcast_in_dim.59), kind=kLoop, calls=%fused_computation.36 | loop fusion | flops 5120000 | bytes 20480128 | tf_op jit(solution)/shard_map/jit(_take)/select_n | solution.py:73
  272.3 17.3 %copy.32 = bf16[128,1,2,96,200]{3,4,2,1,0:T(8,128)(2,1)} copy(bf16[128,1,2,96,200]{4,3,2,1,0:T(8,128)(2,1)} %all-to-all-done.1) | data formatting | bytes 19660800 | tf_op jit(solution)/shard_map/all_to_all | solution.py:32
  289.6 123.4 %all-to-all-done.2 = bf16[128,1,2,104,200]{3,4,2,1,0:T(8,128)(2,1)} async-done(((bf16[128,1,2,104,200]{3,4,2,1,0:T(8,128)(2,1)}), bf16[128,1,2,104,200]{3,4,2,1,0:T(8,128)(2,1)}, u32[]{:S(2)}, u32[]{:S(2)}) %all-to-all-start.2) | async-done | bytes 10649632 | tf_op jit(solution)/shard_map/all_to_all | solution.py:32
  413.1 18.7 %pad_maximum_fusion = bf16[128,1,2,200,200]{3,4,2,1,0:T(8,128)(2,1)} fusion(bf16[128,1,2,104,200]{3,4,2,1,0:T(8,128)(2,1)} %all-to-all-done.2, bf16[128,1,2,96,200]{3,4,2,1,0:T(8,128)(2,1)} %copy.32), kind=kLoop, calls=%fused_computation.34 | loop fusion | flops 40960000 | bytes 40960000 | tf_op jit(solution)/shard_map/concatenate | solution.py:33
  431.7 17.1 %gather_fusion.1 = bf16[128,200,200]{1,2,0:T(8,128)(2,1)} fusion(bf16[256,200,200]{1,2,0:T(8,128)(2,1)} %bitcast.71, s32[1024]{0:T(1024)S(1)} %pad_clamp_fusion.1), kind=kCustom, calls=%fused_computation.1 | custom fusion | bytes 20480512 | tf_op jit(solution)/shard_map/jit(_take)/gather | solution.py:72
  448.9 17.9 %copy.33 = bf16[128,200,200]{2,1,0:T(8,128)(2,1)} copy(bf16[128,200,200]{1,2,0:T(8,128)(2,1)} %gather_fusion.1) | data formatting | bytes 20480000 | tf_op jit(solution)/shard_map/jit(_take)/gather | solution.py:72
  466.8 10.3 %broadcast_select_fusion.2 = bf16[16,8,200,200]{3,2,1,0:T(8,128)(2,1)} fusion(bf16[16,8,200,200]{3,2,1,0:T(8,128)(2,1)} %bitcast.72, pred[16,8]{1,0:T(8,128)(4,1)S(1)} %broadcast_in_dim.51), kind=kLoop, calls=%fused_computation.37 | loop fusion | flops 5120000 | bytes 20480128 | tf_op jit(solution)/shard_map/jit(_take)/select_n | solution.py:72
  477.0 110.3 %while.10 = (s32[]{:T(128)}, f32[16,8,400]{2,1,0:T(8,128)S(1)}, bf16[400,400]{1,0:T(8,128)(2,1)S(1)}, bf16[16,8,200,200]{3,2,1,0:T(8,128)(2,1)}, bf16[16,8,200,2...) while((s32[]{:T(128)}, f32[16,8,400]{2,1,0:T(8,128)S(1)}, bf16[400,400]{1,0:T(8,128)(2,1)S(1)}, ...), condition=%wide.region_6.7_spmd, body=%wide.region_3.6_spmd.sunk | while | flops 1156636800 | bytes 19904180 | solution.py:83
  477.0 1.8 multiply_convert_fusion.2
  482.0 1.9 multiply_reduce_fusion.7
  483.9 1.8 multiply_convert_fusion.2
  488.9 1.9 multiply_reduce_fusion.7
  495.8 1.9 multiply_reduce_fusion.7
  502.7 1.9 multiply_reduce_fusion.7
  509.6 1.9 multiply_reduce_fusion.7
  511.5 1.8 multiply_convert_fusion.2
  516.5 1.9 multiply_reduce_fusion.7
  518.4 1.8 multiply_convert_fusion.2
  523.4 1.9 multiply_reduce_fusion.7
  525.3 1.8 multiply_convert_fusion.2
  530.3 1.9 multiply_reduce_fusion.7
  532.2 1.8 multiply_convert_fusion.2
  537.2 1.9 multiply_reduce_fusion.7
  539.1 1.8 multiply_convert_fusion.2
  544.1 1.9 multiply_reduce_fusion.7
  546.0 1.8 multiply_convert_fusion.2
  551.0 1.9 multiply_reduce_fusion.7
  557.9 1.9 multiply_reduce_fusion.7
  564.8 1.9 multiply_reduce_fusion.7
  571.7 1.9 multiply_reduce_fusion.7
  573.6 1.8 multiply_convert_fusion.2
  578.6 1.9 multiply_reduce_fusion.7
  580.5 1.8 multiply_convert_fusion.2
  585.5 1.9 multiply_reduce_fusion.7
  589.0 11.9 %psum.28 = f32[]{:T(128)} all-reduce(f32[]{:T(128)S(6)} %mul_shard_map.3), channel_id=1, replica_groups=mesh['grp_0'=4,'grp_1'=4,'grp_2'=4,'sub'=2] {'grp_0'}, use_global_device_ids=true, to_apply=%region_9.10 | all-reduce | flops 1 | bytes 8 | tf_op jit(solution)/shard_map/psum | solution.py:38
  600.9 13.8 %psum.29 = f32[]{:T(128)} all-reduce(f32[]{:T(128)} %psum.28), channel_id=1, replica_groups=mesh['grp_0'=4,'grp_1'=4,'grp_2'=4,'sub'=2] {'grp_1'}, use_global_device_ids=true, to_apply=%region_10.11 | all-reduce | flops 1 | bytes 8 | tf_op jit(solution)/shard_map/psum | solution.py:38
  614.7 11.1 %psum.30 = f32[]{:T(128)} all-reduce(f32[]{:T(128)} %psum.29), channel_id=1, replica_groups=mesh['grp_0'=4,'grp_1'=4,'grp_2'=4,'sub'=2] {'grp_2'}, use_global_device_ids=true, to_apply=%region_11.12 | all-reduce | flops 1 | bytes 8 | tf_op jit(solution)/shard_map/psum | solution.py:38
  625.7 9.2 %psum.31 = f32[1]{0:T(128)} all-reduce(f32[1]{0:T(128)} %bitcast.19), channel_id=1, replica_groups=mesh['grp_0'=4,'grp_1'=4,'grp_2'=4,'sub'=2] {'sub'}, use_global_device_ids=true, to_apply=%region_12.13 | all-reduce | flops 1 | bytes 8 | tf_op jit(solution)/shard_map/psum | solution.py:38
  (132 shorter events, 71.2 us)
Async XLA Ops:
  0.6 27.1 %copy-start = (bf16[32,200,200]{2,1,0:T(8,128)(2,1)S(1)}, bf16[32,200,200]{2,1,0:T(8,128)(2,1)}, u32[]{:S(2)}) copy-start(bf16[32,200,200]{2,1,0:T(8,128)(2,1)} %param.6) | copy-start | bytes 7680004
  69.6 157.7 %all-to-all-start.1 = ((bf16[128,1,2,96,200]{4,3,2,1,0:T(8,128)(2,1)}), bf16[128,1,2,96,200]{4,3,2,1,0:T(8,128)(2,1)}, u32[]{:S(2)}, u32[]{:S(2)}) async-start(bf16[128,1,2,96,200]{4,3,2,1,0:T(8,128)(2,1)} %split.8), calls=%async_computation.1 | async-start | bytes 25165824 | tf_op jit(solution)/shard_map/all_to_all | solution.py:32
  227.3 185.7 %all-to-all-start.2 = ((bf16[128,1,2,104,200]{3,4,2,1,0:T(8,128)(2,1)}), bf16[128,1,2,104,200]{3,4,2,1,0:T(8,128)(2,1)}, u32[]{:S(2)}, u32[]{:S(2)}) async-start(bf16[128,1,2,104,200]{3,4,2,1,0:T(8,128)(2,1)} %copy.31), calls=%async_computation.2 | async-start | bytes 26214400 | tf_op jit(solution)/shard_map/all_to_all | solution.py:32
  466.7 10.3 %copy-start.2 = (bf16[400,400]{1,0:T(8,128)(2,1)S(1)}, bf16[400,400]{1,0:T(8,128)(2,1)}, u32[]{:S(2)}) copy-start(bf16[400,400]{1,0:T(8,128)(2,1)} %param.9) | copy-start | bytes 960004
  587.4 48.4 %copy-start.1 = (bf16[32,200,200]{2,1,0:T(8,128)(2,1)S(1)}, bf16[32,200,200]{2,1,0:T(8,128)(2,1)}, u32[]{:S(2)}) copy-start(bf16[32,200,200]{2,1,0:T(8,128)(2,1)} %param.6) | copy-start | bytes 7680004
where the time goes:
time: 639 us; the launch traced here: 636 us
  waiting for transfers between devices  245 us (38%)
  local copies, waits for them, and re-layouts  119 us (19%)
  matrix products  108 us (17%)
  blocking collectives  66.8 us (10%)
  other arithmetic  64.7 us (10%)
  starting transfers between devices  30 us (5%)
    all_to_all x2, waiting for transfers between devices, several_exchanges(): lax.all_to_all(section, axis, split_axis=0, concat_axis=0, tiled=True)  245 us
    psum x4, blocking collectives, over_axes(): value = lax.psum(value, axis)  45.9 us
    split x3, local copies, waits for them, and re-layouts, several_exchanges(): jnp.split(tiles, edges_of(tiles.shape[widest], pieces), axis=widest)  41.9 us
    gather x2, local copies, waits for them, and re-layouts, local(): jnp.take(arrived.reshape(owners * cap, basis, basis), slots, axis=0)  35 us
    all_to_all x2, starting transfers between devices, several_exchanges(): lax.all_to_all(section, axis, split_axis=0, concat_axis=0, tiled=True)  30 us
    dot_general x16, matrix products, block_energies(): jnp.einsum('nab,bk->nak', right, lower, preferred_element_type=jnp.float32)  29.7 us
    dot_general x16, matrix products, block_energies(): jnp.einsum('nab,nbc->nac', left, right, preferred_element_type=jnp.float32)  28.3 us
    dot_general x16, matrix products, block_energies(): jnp.einsum('nab,bk->nak', left, upper, preferred_element_type=jnp.float32)  27.7 us
  transfers between devices with their start and end apart: 2, of which 2 were waited for; matrix products, arithmetic and copies ran while one was open for 11% of the time, Pallas kernels for 0%

commit v1 on v0

--- a/solution.py
+++ b/solution.py
@@ -35,7 +35,7 @@
 
 def over_axes(value, axes):
     for axis in axes:
-        value = lax.psum(value, axis)
+        value = jnp.sum(lax.all_gather(value, axis), axis=0)
     return value
 
 

time: 639 us -> 647 us (1.013)
  local copies, waits for them, and re-layouts: 119 us -> 128 us
    psum x4 -> x0, blocking collectives: 45.9 us -> none  [over_axes(): value = lax.psum(value, axis)]
    unnamed x0 -> x4, blocking collectives: none -> 43.5 us
    unnamed x7 -> x21, local copies, waits for them, and re-layouts: 0.83 us -> 10.1 us
where the time goes in v1:
time: 647 us; the launch traced here: 643 us
  waiting for transfers between devices  243 us (38%)
  local copies, waits for them, and re-layouts  128 us (20%)
  matrix products  108 us (17%)
  other arithmetic  67.1 us (10%)
  blocking collectives  64.4 us (10%)
  starting transfers between devices  30 us (5%)
    all_to_all x2, waiting for transfers between devices, several_exchanges(): lax.all_to_all(section, axis, split_axis=0, concat_axis=0, tiled=True)  243 us
    unnamed x4, blocking collectives  43.5 us
    split x3, local copies, waits for them, and re-layouts, several_exchanges(): jnp.split(tiles, edges_of(tiles.shape[widest], pieces), axis=widest)  41.9 us
    gather x2, local copies, waits for them, and re-layouts, local(): jnp.take(arrived.reshape(owners * cap, basis, basis), slots, axis=0)  34.8 us
    all_to_all x2, starting transfers between devices, several_exchanges(): lax.all_to_all(section, axis, split_axis=0, concat_axis=0, tiled=True)  30 us
    dot_general x16, matrix products, block_energies(): jnp.einsum('nab,bk->nak', right, lower, preferred_element_type=jnp.float32)  29.7 us
    dot_general x16, matrix products, block_energies(): jnp.einsum('nab,nbc->nac', left, right, preferred_element_type=jnp.float32)  28.3 us
    dot_general x16, matrix products, block_energies(): jnp.einsum('nab,bk->nak', left, upper, preferred_element_type=jnp.float32)  27.7 us
  transfers between devices with their start and end apart: 2, of which 2 were waited for; matrix products, arithmetic and copies ran while one was open for 11% of the time, Pallas kernels for 0%

profile of v1, /device:TPU:1, one launch (start us, length us, event | category | flops | bytes accessed | tf_op | source)
XLA Modules:
  0.0 643.5 jit_solution(12241140137679793305)
XLA Ops:
  5.2 20.9 %all_to_all.19 = s32[128,1,2]{2,1,0:T(1,128)S(1)} all-to-all(s32[128,1,2]{2,1,0:T(1,128)S(1)} %bitcast.84), channel_id=1, replica_groups=mesh['grp_0'=4,'grp_1'=4,'grp_2'=4,'sub'=2] {'grp_0','grp_1','grp_2','sub'}, dimensions={0} | all-to-all | bytes 2048 | tf_op jit(solution)/shard_map/all_to_all | solution.py:67
  27.8 12.6 %gather_fusion = bf16[256,200,200]{2,1,0:T(8,128)(2,1)} fusion(bf16[32,200,200]{2,1,0:T(8,128)(2,1)S(1)} %copy-done, s32[1024]{0:T(1024)S(1)} %pad_clamp_fusion.2), kind=kCustom, calls=%fused_computation | custom fusion | bytes 40961024 | tf_op jit(solution)/shard_map/jit(_take)/gather | solution.py:70
  40.4 18.3 %broadcast_select_fusion = bf16[128,1,2,200,200]{4,3,2,1,0:T(8,128)(2,1)} fusion(bf16[128,1,2,200,200]{4,3,2,1,0:T(8,128)(2,1)} %bitcast.78, pred[128,2]{1,0:T(8,128)(4,1)S(1)} %compare_and_fusion), kind=kLoop, calls=%fused_computation.35 | loop fusion | flops 10240000 | bytes 40960256 | tf_op jit(solution)/shard_map/jit(_take)/select_n | solution.py:70
  58.7 11.0 %split.8 = bf16[128,1,2,96,200]{4,3,2,1,0:T(8,128)(2,1)} slice(bf16[128,1,2,200,200]{4,3,2,1,0:T(8,128)(2,1)} %broadcast_select_fusion), slice={[0:128], [0:1], [0:2], [0:96], [0:200]} | slice | bytes 19660800 | tf_op jit(solution)/shard_map/split | solution.py:30
  69.6 5.5 all-to-all-start.1
  75.1 12.2 %split.9 = bf16[128,1,2,104,200]{4,3,2,1,0:T(8,128)(2,1)} slice(bf16[128,1,2,200,200]{4,3,2,1,0:T(8,128)(2,1)} %broadcast_select_fusion), slice={[0:128], [0:1], [0:2], [96:200], [0:200]} | slice | bytes 21299200 | tf_op jit(solution)/shard_map/split | solution.py:30
  87.3 18.8 %copy.31 = bf16[128,1,2,104,200]{3,4,2,1,0:T(8,128)(2,1)} copy(bf16[128,1,2,104,200]{4,3,2,1,0:T(8,128)(2,1)} %split.9) | data formatting | bytes 21299200 | tf_op jit(solution)/shard_map/split | solution.py:30
  106.1 121.2 %all-to-all-done.1 = bf16[128,1,2,96,200]{4,3,2,1,0:T(8,128)(2,1)} async-done(((bf16[128,1,2,96,200]{4,3,2,1,0:T(8,128)(2,1)}), bf16[128,1,2,96,200]{4,3,2,1,0:T(8,128)(2,1)}, u32[]{:S(2)}, u32[]{:S(2)}) %all-to-all-start.1) | async-done | bytes 9830432 | tf_op jit(solution)/shard_map/all_to_all | solution.py:32
  227.3 24.5 %all-to-all-start.2 = ((bf16[128,1,2,104,200]{3,4,2,1,0:T(8,128)(2,1)}), bf16[128,1,2,104,200]{3,4,2,1,0:T(8,128)(2,1)}, u32[]{:S(2)}, u32[]{:S(2)}) async-start(bf16[128,1,2,104,200]{3,4,2,1,0:T(8,128)(2,1)} %copy.31), calls=%async_computation.2 | async-start | bytes 26214400 | tf_op jit(solution)/shard_map/all_to_all | solution.py:32
  252.6 8.7 %gather_fusion.2 = bf16[128,200,200]{2,1,0:T(8,128)(2,1)} fusion(bf16[32,200,200]{2,1,0:T(8,128)(2,1)S(1)} %copy-done, s32[1024]{0:T(1024)S(1)} %pad_clamp_fusion), kind=kCustom, calls=%fused_computation.2 | custom fusion | bytes 20480512 | tf_op jit(solution)/shard_map/jit(_take)/gather | solution.py:73
  263.4 10.1 %broadcast_select_fusion.1 = bf16[16,8,200,200]{3,2,1,0:T(8,128)(2,1)} fusion(bf16[16,8,200,200]{3,2,1,0:T(8,128)(2,1)} %bitcast.81, pred[16,8]{1,0:T(8,128)(4,1)S(1)} %broadcast_in_dim.59), kind=kLoop, calls=%fused_computation.36 | loop fusion | flops 5120000 | bytes 20480128 | tf_op jit(solution)/shard_map/jit(_take)/select_n | solution.py:73
  273.5 17.3 %copy.32 = bf16[128,1,2,96,200]{3,4,2,1,0:T(8,128)(2,1)} copy(bf16[128,1,2,96,200]{4,3,2,1,0:T(8,128)(2,1)} %all-to-all-done.1) | data formatting | bytes 19660800 | tf_op jit(solution)/shard_map/all_to_all | solution.py:32
  290.9 122.2 %all-to-all-done.2 = bf16[128,1,2,104,200]{3,4,2,1,0:T(8,128)(2,1)} async-done(((bf16[128,1,2,104,200]{3,4,2,1,0:T(8,128)(2,1)}), bf16[128,1,2,104,200]{3,4,2,1,0:T(8,128)(2,1)}, u32[]{:S(2)}, u32[]{:S(2)}) %all-to-all-start.2) | async-done | bytes 10649632 | tf_op jit(solution)/shard_map/all_to_all | solution.py:32
  413.1 18.7 %pad_maximum_fusion = bf16[128,1,2,200,200]{3,4,2,1,0:T(8,128)(2,1)} fusion(bf16[128,1,2,104,200]{3,4,2,1,0:T(8,128)(2,1)} %all-to-all-done.2, bf16[128,1,2,96,200]{3,4,2,1,0:T(8,128)(2,1)} %copy.32), kind=kLoop, calls=%fused_computation.34 | loop fusion | flops 40960000 | bytes 40960000 | tf_op jit(solution)/shard_map/concatenate | solution.py:33
  431.7 17.1 %gather_fusion.1 = bf16[128,200,200]{1,2,0:T(8,128)(2,1)} fusion(bf16[256,200,200]{1,2,0:T(8,128)(2,1)} %bitcast.79, s32[1024]{0:T(1024)S(1)} %pad_clamp_fusion.1), kind=kCustom, calls=%fused_computation.1 | custom fusion | bytes 20480512 | tf_op jit(solution)/shard_map/jit(_take)/gather | solution.py:72
  448.9 17.7 %copy.33 = bf16[128,200,200]{2,1,0:T(8,128)(2,1)} copy(bf16[128,200,200]{1,2,0:T(8,128)(2,1)} %gather_fusion.1) | data formatting | bytes 20480000 | tf_op jit(solution)/shard_map/jit(_take)/gather | solution.py:72
  466.5 10.2 %broadcast_select_fusion.2 = bf16[16,8,200,200]{3,2,1,0:T(8,128)(2,1)} fusion(bf16[16,8,200,200]{3,2,1,0:T(8,128)(2,1)} %bitcast.80, pred[16,8]{1,0:T(8,128)(4,1)S(1)} %broadcast_in_dim.51), kind=kLoop, calls=%fused_computation.37 | loop fusion | flops 5120000 | bytes 20480128 | tf_op jit(solution)/shard_map/jit(_take)/select_n | solution.py:72
  476.8 110.3 %while.10 = (s32[]{:T(128)}, f32[16,8,400]{2,1,0:T(8,128)S(1)}, bf16[400,400]{1,0:T(8,128)(2,1)S(1)}, bf16[16,8,200,200]{3,2,1,0:T(8,128)(2,1)}, bf16[16,8,200,2...) while((s32[]{:T(128)}, f32[16,8,400]{2,1,0:T(8,128)S(1)}, bf16[400,400]{1,0:T(8,128)(2,1)S(1)}, ...), condition=%wide.region_6.7_spmd, body=%wide.region_3.6_spmd.sunk | while | flops 1156636800 | bytes 19904180 | solution.py:83
  476.8 1.8 multiply_convert_fusion.2
  481.8 1.9 multiply_reduce_fusion.7
  483.7 1.8 multiply_convert_fusion.2
  488.7 1.9 multiply_reduce_fusion.7
  490.6 1.8 multiply_convert_fusion.2
  495.6 1.9 multiply_reduce_fusion.7
  497.5 1.8 multiply_convert_fusion.2
  502.5 1.9 multiply_reduce_fusion.7
  504.4 1.8 multiply_convert_fusion.2
  509.4 1.9 multiply_reduce_fusion.7
  511.3 1.8 multiply_convert_fusion.2
  516.2 1.9 multiply_reduce_fusion.7
  518.2 1.8 multiply_convert_fusion.2
  523.1 1.9 multiply_reduce_fusion.7
  530.0 1.9 multiply_reduce_fusion.7
  536.9 1.9 multiply_reduce_fusion.7
  543.8 1.9 multiply_reduce_fusion.7
  545.7 1.8 multiply_convert_fusion.2
  550.7 1.9 multiply_reduce_fusion.7
  552.6 1.8 multiply_convert_fusion.2
  557.6 1.9 multiply_reduce_fusion.7
  559.5 1.8 multiply_convert_fusion.2
  564.5 1.9 multiply_reduce_fusion.7
  571.4 1.9 multiply_reduce_fusion.7
  578.3 1.9 multiply_reduce_fusion.7
  585.2 1.9 multiply_reduce_fusion.7
  590.8 11.3 %all-reduce = f32[4]{0:T(128)S(1)} all-reduce(f32[4]{0:T(128)S(1)} %dynamic-update-slice), channel_id=1, replica_groups=mesh['grp_0'=4,'grp_1'=4,'grp_2'=4,'sub'=2] {'grp_0'}, use_global_device_ids=true, to_apply=%add | all-reduce | flops 4 | bytes 32
  605.3 13.2 %all-reduce.1 = f32[4]{0:T(128)S(1)} all-reduce(f32[4]{0:T(128)S(1)} %dynamic-update-slice.1), channel_id=1, replica_groups=mesh['grp_0'=4,'grp_1'=4,'grp_2'=4,'sub'=2] {'grp_1'}, use_global_device_ids=true, to_apply=%add.1 | all-reduce | flops 4 | bytes 32
  621.1 10.4 %all-reduce.2 = f32[4]{0:T(128)S(1)} all-reduce(f32[4]{0:T(128)S(1)} %dynamic-update-slice.2), channel_id=1, replica_groups=mesh['grp_0'=4,'grp_1'=4,'grp_2'=4,'sub'=2] {'grp_2'}, use_global_device_ids=true, to_apply=%add.2 | all-reduce | flops 4 | bytes 32
  633.5 8.6 %all-reduce.3 = f32[2]{0:T(128)S(1)} all-reduce(f32[2]{0:T(128)S(1)} %dynamic-update-slice.3), channel_id=1, replica_groups=mesh['grp_0'=4,'grp_1'=4,'grp_2'=4,'sub'=2] {'sub'}, use_global_device_ids=true, to_apply=%add.3 | all-reduce | flops 2 | bytes 16
  (150 shorter events, 82.9 us)
Async XLA Ops:
  0.6 27.1 %copy-start = (bf16[32,200,200]{2,1,0:T(8,128)(2,1)S(1)}, bf16[32,200,200]{2,1,0:T(8,128)(2,1)}, u32[]{:S(2)}) copy-start(bf16[32,200,200]{2,1,0:T(8,128)(2,1)} %param.6) | copy-start | bytes 7680004
  69.6 157.7 %all-to-all-start.1 = ((bf16[128,1,2,96,200]{4,3,2,1,0:T(8,128)(2,1)}), bf16[128,1,2,96,200]{4,3,2,1,0:T(8,128)(2,1)}, u32[]{:S(2)}, u32[]{:S(2)}) async-start(bf16[128,1,2,96,200]{4,3,2,1,0:T(8,128)(2,1)} %split.8), calls=%async_computation.1 | async-start | bytes 25165824 | tf_op jit(solution)/shard_map/all_to_all | solution.py:32
  227.3 185.7 %all-to-all-start.2 = ((bf16[128,1,2,104,200]{3,4,2,1,0:T(8,128)(2,1)}), bf16[128,1,2,104,200]{3,4,2,1,0:T(8,128)(2,1)}, u32[]{:S(2)}, u32[]{:S(2)}) async-start(bf16[128,1,2,104,200]{3,4,2,1,0:T(8,128)(2,1)} %copy.31), calls=%async_computation.2 | async-start | bytes 26214400 | tf_op jit(solution)/shard_map/all_to_all | solution.py:32
  466.5 10.2 %copy-start.2 = (bf16[400,400]{1,0:T(8,128)(2,1)S(1)}, bf16[400,400]{1,0:T(8,128)(2,1)}, u32[]{:S(2)}) copy-start(bf16[400,400]{1,0:T(8,128)(2,1)} %param.9) | copy-start | bytes 960004
  476.8 143.8 %copy-start.3 = (u32[128]{0:T(128)S(1)}, u32[128]{0:T(128)}, u32[]{:S(2)}) copy-start(u32[128]{0:T(128)} %constant.153) | copy-start | bytes 1540
  587.1 56.4 %copy-start.1 = (bf16[32,200,200]{2,1,0:T(8,128)(2,1)S(1)}, bf16[32,200,200]{2,1,0:T(8,128)(2,1)}, u32[]{:S(2)}) copy-start(bf16[32,200,200]{2,1,0:T(8,128)(2,1)} %param.6) | copy-start | bytes 7680004
